TPU v7x, 32 devices: a whole 2x2x4 slice. The times are simulated.
32 devices in a mesh: groups: 2 (over y), expert: 16 (over z, x, core).
Axes of the slice: x: 2, y: 2, z: 4, core: 2. Of those that a mesh axis runs over, the one named last changes fastest.
Arguments:
- activations: bfloat16 [2, 512, 2048], P(None, ('groups', 'expert')), parts along dimension 1, may hold values from -6 to 6
- pick_weight: float32 [2, 512, 1], P(None, ('groups', 'expert')), parts along dimension 1, may hold values from 0.2 to 1
- expert_ids: int32 [2, 512, 1], P(None, ('groups', 'expert')), parts along dimension 1, may hold values from 0 to 7, as said below
- replica: int32 [2, 512, 1], P(None, ('groups', 'expert')), parts along dimension 1, may hold values from 0 to 4, as said below
- old_home: int32 [8], replicated, may hold values from 0 to 7, each once
- new_expert: int32 [32], P('groups'), parts along dimension 0, may hold values from 0 to 7, as said below
- gate_panel: bfloat16 [16, 2048, 384], P('expert'), may hold values from -0.125 to 0.125
- up_panel: bfloat16 [16, 2048, 384], P('expert'), may hold values from -0.125 to 0.125
- down_panel: bfloat16 [16, 2048, 384], P('expert'), may hold values from -0.21875 to 0.21875
Outputs:
- layer_output: bfloat16 [2, 512, 2048], P(None, ('groups', 'expert')), parts along dimension 1
- slot_load: int32 [32], P(('groups', 'expert')), parts along dimension 0
There are 2 independent parts, one for each index of `groups`. A program takes and returns all parts, laid end to end along the dimension named above; an argument that names none is the same for every part. Nothing has to cross between parts.
Inputs may be any that keep to these rules, and one draw needn't show every extreme that they name: `new_expert`: every expert is held by 1 or 5 slots. `expert_ids`: the 1 expert that a token names are different. replica[s, t, k] is below the number of slots that new_expert gives to expert_ids[s, t, k]. The picks of the 16 tokens of one device in one batch that land on one slot number at most 2, and in each batch some slot receives exactly 2 from every device.
All inputs are finite; a program needn't handle non-finite values.
Results may differ from a plain program's by a relative error of at most 0.0057.
Values may be sent and summed in bfloat16 or wider, within the bound.
No kernel may reach another device: no remote copies, remote signals or barrier semaphores. Data moves between devices by JAX's collectives and lax.ppermute only.
A program may use at most 128 MiB of HBM per device.

v0:
```python
import jax
import jax.numpy as jnp
from jax import lax
from jax.sharding import PartitionSpec as P

LANES = 128


def slot_rank(new_expert, me):
    positions = jnp.arange(new_expert.shape[0], dtype=jnp.int32)
    mine = jnp.sum(jnp.where(positions == me, new_expert, 0))
    rank = jnp.sum(((new_expert == mine) & (positions < me)).astype(jnp.int32))
    return (mine, rank)


def per_device(
    activations,
    pick_weight,
    expert_ids,
    replica,
    old_home,
    new_expert,
    gate_panel,
    up_panel,
    down_panel,
):
    me = lax.axis_index("expert")
    batches, tokens, width = activations.shape
    top = expert_ids.shape[2]
    rows = batches * tokens
    x = activations.reshape(rows, width)
    picks = jnp.concatenate([expert_ids.reshape(rows, top), replica.reshape(rows, top)], axis=1)
    weights = pick_weight.reshape(rows, top)
    picks_all = lax.all_gather(picks, "expert", axis=0, tiled=True)
    weights_all = lax.all_gather(weights, "expert", axis=0, tiled=True)
    x_all = lax.all_gather(x, "expert", axis=0, tiled=True)
    ids_all = picks_all[:, :top]
    rep_all = picks_all[:, top:]
    mine, rank = slot_rank(new_expert, me)
    load = jnp.sum(((ids_all == mine) & (rep_all == rank)).astype(jnp.int32))
    labels = jnp.arange(old_home.shape[0], dtype=jnp.int32)
    held = jnp.sum(jnp.where(old_home == me // 2, labels, 0))
    scale = jnp.sum(jnp.where(ids_all == held, weights_all, 0.0), axis=1, keepdims=True)
    gate = jnp.dot(x_all, gate_panel[0], preferred_element_type=jnp.float32)
    up = jnp.dot(x_all, up_panel[0], preferred_element_type=jnp.float32)
    hidden = (jax.nn.silu(gate) * up).astype(jnp.bfloat16)
    part = lax.dot_general(
        hidden, down_panel[0], (((1,), (1,)), ((), ())), preferred_element_type=jnp.float32
    )
    part = (part * scale).astype(jnp.bfloat16)
    total = lax.psum_scatter(part, "expert", scatter_dimension=0, tiled=True)
    return (total.reshape(batches, tokens, width), load.reshape(1))


def solution(mesh):
    return jax.shard_map(
        per_device,
        mesh=mesh,
        in_specs=(
            P(None, ("groups", "expert"), None),
            P(None, ("groups", "expert"), None),
            P(None, ("groups", "expert"), None),
            P(None, ("groups", "expert"), None),
            P(),
            P("groups"),
            P("expert", None, None),
            P("expert", None, None),
            P("expert", None, None),
        ),
        out_specs=(P(None, ("groups", "expert"), None), P(("groups", "expert"))),
        check_vma=False,
    )
```

profile of v0, /device:TPU:0, one launch (start us, length us, event | category | flops | bytes accessed | tf_op | source)
XLA Modules:
  0.0 146.4 jit_solution(16085344382893016342)
XLA Ops:
  7.2 0.0 copy-start
  7.2 0.0 all-gather.3.cloned.1.call-start
  7.2 0.7 all-gather.3.cloned.1.call-update
  7.9 0.0 reduce-scatter.2.cloned.1.call-start
  8.0 0.5 broadcast.13
  8.5 1.3 reduce.9
  9.8 0.1 reshape.30
  9.9 0.5 broadcast.14
  10.4 1.3 reduce.11
  11.8 0.1 reshape.25
  11.8 1.3 reduce.10
  13.2 0.1 reshape.26
  13.3 23.1 %all-gather = s32[16,32,2]{1,2,0:T(2,128)S(1)} all-gather(s32[1,32,2]{1,2,0:T(2,128)S(1)} %add_bitcast_fusion), channel_id=1, replica_groups=mesh['groups'=2,'expert'=16] {'expert'}, dimensions={0}, use_global_device_ids=true | all-gather | bytes 4352 | tf_op jit(solution)/shard_map/all_gather | solution.py:34
  36.4 0.1 reshape.34
  36.5 1.2 dynamic-slice
  38.4 0.2 dynamic-update-slice
  38.6 29.9 %all-reduce = f32[512]{0:T(512)S(1)} all-reduce(f32[512]{0:T(512)S(1)} %dynamic-update-slice), channel_id=1, replica_groups=mesh['groups'=2,'expert'=16] {'expert'}, use_global_device_ids=true, to_apply=%add | all-reduce | flops 512 | bytes 4096
  68.5 1.3 fusion.20
  69.8 0.6 compare_select_fusion
  70.5 0.0 copy-start.2
  70.5 0.0 all-gather.3.cloned.1.call-done
  70.5 4.3 %fusion.3 = f32[512,384]{1,0:T(8,128)} fusion(bf16[512,2048]{1,0:T(8,128)(2,1)} %all-gather.3.cloned.1.call-done, bf16[1,2048,384]{2,1,0:T(8,128)(2,1)} %param.15), kind=kOutput, calls=%fused_computation.4 | convolution fusion | flops 805306368 | bytes 4456448 | tf_op jit(solution)/shard_map/dot_general | solution.py:44
  74.8 0.0 copy-done
  74.8 0.0 copy-done.2
  74.8 5.5 %multiply_convert_fusion = bf16[512,2048]{1,0:T(8,128)(2,1)} fusion(f32[512]{0:T(512)S(1)} %bitcast.32, bf16[1,2048,384]{2,1,0:T(8,128)(2,1)S(1)} %copy-done, bf16[512,2048]{1,0:T(8,128)(2,1)} %all-gather.3.cloned.1.call-done, bf16[1,2048,384]{2,1,0:T(8,128)(2,1)S(1)} %copy-done.2, f32[512,384]{1,0:T(8,128)} %fusion.3), kind=kOutput, calls=%fused_computation | convolution fusion | flops 1613889536 | bytes 8128512 | tf_op jit(solution)/shard_map/dot_general | solution.py:47
  80.3 0.0 copy-start.1
  80.3 0.0 reduce-scatter.2.cloned.1.call-update
  80.3 0.6 copy-done.1
  81.0 0.6 fusion.21
  81.6 1.3 fusion.22
  82.9 1.9 %fusion.19 = s32[]{:T(128)} fusion(s32[512,2]{0,1:T(2,128)S(1)} %reshape.34, s32[]{:T(128)} %fusion.22, s32[]{:T(128)} %fusion.21), kind=kLoop, calls=%fused_computation.19 | loop fusion | flops 2559 | bytes 4108 | tf_op jit(solution)/shard_map/reduce_sum | solution.py:40
  84.7 54.9 %reduce-scatter.2.cloned.1.call-done = bf16[32,2048]{1,0:T(8,128)(2,1)} async-done(((bf16[512,2048]{1,0:T(8,128)(2,1)}), bf16[32,2048]{1,0:T(8,128)(2,1)}) %reduce-scatter.2.cloned.1.call-update) | async-done | bytes 131088 | tf_op jit(solution)/shard_map/reduce_scatter | solution.py:51
  (3 shorter events, 0.0 us)
Async XLA Ops:
  7.2 67.7 %copy-start = (bf16[1,2048,384]{2,1,0:T(8,128)(2,1)S(1)}, bf16[1,2048,384]{2,1,0:T(8,128)(2,1)}, u32[]{:S(2)}) copy-start(bf16[1,2048,384]{2,1,0:T(8,128)(2,1)} %param.17) | copy-start | bytes 4718596
  7.2 63.3 %all-gather.3.cloned.1.call-start = ((), (), s32[]{:S(2)}) async-start(), calls=%async_computation.1 | async-start | bytes 2228224 | tf_op jit(solution)/shard_map/all_gather | solution.py:36
  7.9 131.7 %reduce-scatter.2.cloned.1.call-start = ((), (), s32[]{:S(2)}) async-start(), calls=%async_computation.2 | async-start | bytes 2228224 | tf_op jit(solution)/shard_map/reduce_scatter | solution.py:51
  70.5 4.3 %copy-start.2 = (bf16[1,2048,384]{2,1,0:T(8,128)(2,1)S(1)}, bf16[1,2048,384]{2,1,0:T(8,128)(2,1)}, u32[]{:S(2)}) copy-start(bf16[1,2048,384]{2,1,0:T(8,128)(2,1)} %param.16) | copy-start | bytes 4718596
  80.3 0.7 copy-start.1
Sparse Core Ops, SparseCore 0:
  10.1 44.4 all-gather.2
  80.4 59.1 reduce-scatter.1
where the time goes:
time: 147 us; the launch traced here: 146 us
  waiting for transfers between devices  55.6 us (38%)
  blocking collectives  53 us (36%)
  between operations  14.7 us (10%)
  matrix products  9.76 us (7%)
  other arithmetic  9.75 us (7%)
  local copies, waits for them, and re-layouts  3.49 us (2%)
    reduce_scatter x1, waiting for transfers between devices, per_device(): total = lax.psum_scatter(part, 'expert', scatter_dimension=0, tiled=True)  54.9 us
    unnamed x1, blocking collectives  29.9 us
    all_gather x1, blocking collectives, per_device(): picks_all = lax.all_gather(picks, 'expert', axis=0, tiled=True)  23.1 us
    dot_general x1, matrix products, per_device(): lax.dot_general(hidden, down_panel[0], (((1,), (1,)), ((), ())), preferre...  5.48 us
    dot_general x1, matrix products, per_device(): gate = jnp.dot(x_all, gate_panel[0], preferred_element_type=jnp.float32)  4.28 us
    unnamed x4, other arithmetic  4.04 us
    unnamed x13, local copies, waits for them, and re-layouts  3.32 us
  transfers between devices with their start and end apart: 2, of which 1 were waited for; matrix products, arithmetic and copies ran while one was open for 9% of the time, Pallas kernels for 0%

commit v1 on v0

--- a/solution.py
+++ b/solution.py
@@ -2,8 +2,14 @@
 import jax.numpy as jnp
 from jax import lax
 from jax.sharding import PartitionSpec as P
+from jax.lax import all_gather
 
 LANES = 128
+
+
+def _update_targets(t0, patch, bus_axis):
+    r1 = jnp.concatenate([t0, patch], axis=1)
+    return jnp.split(all_gather(r1, axis=0, axis_name=bus_axis, tiled=True), [t0.shape[1]], axis=1)
 
 
 def slot_rank(new_expert, me):
@@ -31,8 +37,7 @@
     x = activations.reshape(rows, width)
     picks = jnp.concatenate([expert_ids.reshape(rows, top), replica.reshape(rows, top)], axis=1)
     weights = pick_weight.reshape(rows, top)
-    picks_all = lax.all_gather(picks, "expert", axis=0, tiled=True)
-    weights_all = lax.all_gather(weights, "expert", axis=0, tiled=True)
+    picks_all, weights_all = _update_targets(picks, weights, "expert")
     x_all = lax.all_gather(x, "expert", axis=0, tiled=True)
     ids_all = picks_all[:, :top]
     rep_all = picks_all[:, top:]

time: 147 us -> 132 us (0.90)
  blocking collectives: 53 us -> 23.2 us
  waiting for transfers between devices: 55.6 us -> 72.8 us
  other arithmetic: 9.75 us -> 7.91 us
  local copies, waits for them, and re-layouts: 3.49 us -> 2.01 us
    unnamed x1 -> x0, blocking collectives: 29.9 us -> none
    all_gather x1, waiting for transfers between devices: 0.02 us -> 15.9 us  [per_device(): x_all = lax.all_gather(x, 'expert', axis=0, tiled=True)]
    unnamed x13 -> x9, local copies, waits for them, and re-layouts: 3.32 us -> 1.75 us
  transfers between devices with their start and end apart: 2 -> 2, of which waited for: 1 -> 2; matrix products, arithmetic and copies ran while one was open for 9% -> 7% of each run, Pallas kernels for 0% -> 0%
where the time goes in v1:
time: 132 us
  waiting for transfers between devices  72.8 us (55%)
  blocking collectives  23.2 us (18%)
  between operations  16 us (12%)
  matrix products  9.64 us (7%)
  other arithmetic  7.91 us (6%)
  local copies, waits for them, and re-layouts  2.01 us (2%)
    reduce_scatter x1, waiting for transfers between devices, per_device(): total = lax.psum_scatter(part, 'expert', scatter_dimension=0, tiled=True)  56.2 us
    all_gather x1, blocking collectives, _update_targets(): all_gather(r1, axis=0, axis_name=bus_axis, tiled=True)  23.2 us
    all_gather x1, waiting for transfers between devices, per_device(): x_all = lax.all_gather(x, 'expert', axis=0, tiled=True)  15.9 us
    dot_general x1, matrix products, per_device(): lax.dot_general(hidden, down_panel[0], (((1,), (1,)), ((), ())), preferre...  5.47 us
    dot_general x1, matrix products, per_device(): gate = jnp.dot(x_all, gate_panel[0], preferred_element_type=jnp.float32)  4.17 us
    unnamed x4, other arithmetic  4.04 us
  transfers between devices with their start and end apart: 2, of which 2 were waited for; matrix products, arithmetic and copies ran while one was open for 7% of the time, Pallas kernels for 0%

profile of v1, /device:TPU:0, one launch (start us, length us, event | category | flops | bytes accessed | tf_op | source)
XLA Modules:
  0.0 131.7 jit_solution(4512099554793151158)
XLA Ops:
  7.2 0.0 copy-start
  7.2 0.0 all-gather.3.cloned.1.call-start
  7.2 0.7 all-gather.3.cloned.1.call-update
  7.9 0.0 reduce-scatter.2.cloned.1.call-start
  8.0 1.3 fusion.20
  9.9 0.5 broadcast.15
  10.4 1.3 %reduce.9 = f32[2,16]{1,0:T(2,128)S(1)} reduce(f32[2,16,1]{1,2,0:T(1,128)} %param.10, f32[]{:T(128)} %broadcast.15), dimensions={2}, to_apply=%param.10.reduce_sub_computation.3 | reduce | bytes 260 | tf_op args[1]
  11.8 0.1 reshape.27
  11.9 0.5 broadcast.16
  12.4 1.3 %reduce.11 = s32[2,16]{1,0:T(2,128)S(1)} reduce(s32[2,16,1]{1,2,0:T(1,128)} %param.11, s32[]{:T(128)} %broadcast.16), dimensions={2}, to_apply=%param.11.reduce_sub_computation.3 | reduce | bytes 260 | tf_op args[2]
  13.7 0.1 reshape.25
  13.8 1.3 %reduce.10 = s32[2,16]{1,0:T(2,128)S(1)} reduce(s32[2,16,1]{1,2,0:T(1,128)} %param.12, s32[]{:T(128)} %broadcast.16), dimensions={2}, to_apply=%param.12.reduce_sub_computation.3 | reduce | bytes 260 | tf_op args[3]
  15.1 0.1 reshape.26
  15.2 23.2 %all-gather = f32[16,32,3]{1,2,0:T(4,128)S(1)} all-gather(f32[1,32,3]{1,2,0:T(4,128)S(1)} %maximum_bitcast_fusion), channel_id=1, replica_groups=mesh['groups'=2,'expert'=16] {'expert'}, dimensions={0}, use_global_device_ids=true | all-gather | bytes 6528 | tf_op jit(solution)/shard_map/all_gather | solution.py:12
  38.5 0.1 reshape.31
  38.6 0.0 copy-start.2
  38.6 15.9 %all-gather.3.cloned.1.call-done = bf16[512,2048]{1,0:T(8,128)(2,1)} async-done(((bf16[32,2048]{1,0:T(8,128)(2,1)}), bf16[512,2048]{1,0:T(8,128)(2,1)}) %all-gather.3.cloned.1.call-update) | async-done | bytes 2097168 | tf_op jit(solution)/shard_map/all_gather | solution.py:41
  54.5 4.2 %fusion.3 = f32[512,384]{1,0:T(8,128)} fusion(bf16[512,2048]{1,0:T(8,128)(2,1)} %all-gather.3.cloned.1.call-done, bf16[1,2048,384]{2,1,0:T(8,128)(2,1)} %param.15), kind=kOutput, calls=%fused_computation.4 | convolution fusion | flops 805306368 | bytes 4456448 | tf_op jit(solution)/shard_map/dot_general | solution.py:49
  58.6 0.0 copy-done
  58.6 0.0 copy-done.2
  58.6 5.5 %multiply_convert_fusion = bf16[512,2048]{1,0:T(8,128)(2,1)} fusion(f32[512]{0:T(512)S(1)} %bitcast.29, bf16[1,2048,384]{2,1,0:T(8,128)(2,1)S(1)} %copy-done, bf16[512,2048]{1,0:T(8,128)(2,1)} %all-gather.3.cloned.1.call-done, bf16[1,2048,384]{2,1,0:T(8,128)(2,1)S(1)} %copy-done.2, f32[512,384]{1,0:T(8,128)} %fusion.3), kind=kOutput, calls=%fused_computation | convolution fusion | flops 1613889536 | bytes 8128512 | tf_op jit(solution)/shard_map/dot_general | solution.py:52
  64.1 0.0 copy-start.1
  64.1 0.0 reduce-scatter.2.cloned.1.call-update
  64.1 0.6 copy-done.1
  64.8 0.6 fusion.21
  66.1 1.3 fusion.22
  68.0 0.6 fusion.19
  68.6 56.2 %reduce-scatter.2.cloned.1.call-done = bf16[32,2048]{1,0:T(8,128)(2,1)} async-done(((bf16[512,2048]{1,0:T(8,128)(2,1)}), bf16[32,2048]{1,0:T(8,128)(2,1)}) %reduce-scatter.2.cloned.1.call-update) | async-done | bytes 131088 | tf_op jit(solution)/shard_map/reduce_scatter | solution.py:56
  (4 shorter events, 0.0 us)
Async XLA Ops:
  7.2 51.5 %copy-start = (bf16[1,2048,384]{2,1,0:T(8,128)(2,1)S(1)}, bf16[1,2048,384]{2,1,0:T(8,128)(2,1)}, u32[]{:S(2)}) copy-start(bf16[1,2048,384]{2,1,0:T(8,128)(2,1)} %param.17) | copy-start | bytes 4718596
  7.2 47.3 %all-gather.3.cloned.1.call-start = ((), (), s32[]{:S(2)}) async-start(), calls=%async_computation.1 | async-start | bytes 2228224 | tf_op jit(solution)/shard_map/all_gather | solution.py:41
  7.9 116.9 %reduce-scatter.2.cloned.1.call-start = ((), (), s32[]{:S(2)}) async-start(), calls=%async_computation.2 | async-start | bytes 2228224 | tf_op jit(solution)/shard_map/reduce_scatter | solution.py:56
  38.6 20.1 %copy-start.2 = (bf16[1,2048,384]{2,1,0:T(8,128)(2,1)S(1)}, bf16[1,2048,384]{2,1,0:T(8,128)(2,1)}, u32[]{:S(2)}) copy-start(bf16[1,2048,384]{2,1,0:T(8,128)(2,1)} %param.16) | copy-start | bytes 4718596
  64.1 0.7 copy-start.1
Sparse Core Ops, SparseCore 0:
  10.1 44.2 all-gather.2
  64.3 60.5 reduce-scatter.1
